TPU v7x, 32 devices: a whole 2x2x4 slice. The times are simulated.
32 devices in a mesh: row: 4 (over x, core), col: 8 (over z, y).
Axes of the slice: x: 2, y: 2, z: 4, core: 2. Of those that a mesh axis runs over, the one named last changes fastest.
Arguments:
- centres: float32 [65536, 64], P(('row', 'col')), may hold values from -6 to 6
- weights: float32 [65536, 64], P(('row', 'col')), may hold values from -0.25 to 0.25
- targets: float32 [512, 64], replicated, may hold values from -6 to 6
- batch_index: int32 [512], replicated, may hold values from 0 to 65535
- nystrom_index: int32 [4096], replicated, may hold values from 0 to 65535
- eigvecs: float32 [4096, 1024], P('row', 'col'), may hold values from -0.09375 to 0.09375
- mode_scale: float32 [1024], P('col'), may hold values from 0.02 to 0.2
Outputs:
- residual: float32 [512, 64], replicated
- step: float32 [65536, 64], P(('row', 'col'))
All inputs are finite; a program needn't handle non-finite values.
Results may differ from a plain program's by a relative error of at most 0.0001.
Values sent between devices are 32-bit elements; how exact they have to be, the bound alone decides.
A program may use at most 128 MiB of HBM per device.

v0:
```python
import functools
import math

import jax
import jax.numpy as jnp
from jax import lax
from jax.experimental import pallas as pl
from jax.experimental.pallas import tpu as pltpu
from jax.sharding import PartitionSpec as P

learning_rate = 0.25
CORES = 2
HALVES = 2
MESH = pl.DeviceIdType.MESH
VMEM = pl.BlockSpec(memory_space=pltpu.VMEM)
BF16 = jnp.bfloat16
F32 = jnp.float32


def pieces(value, count):
    parts = []
    for step in range(count):
        part = value.astype(BF16).astype(F32)
        parts.append(part)
        value = value - part
    return parts


def paired(value):
    return jnp.concatenate(pieces(value, 2), axis=0).astype(BF16)


def augmented(feats, left):
    width, count = feats.shape
    unit = math.log2(math.e) / width
    square = pieces(-unit * jnp.sum(feats * feats, axis=0, keepdims=True), 3)
    if left:
        high, low = pieces(feats * (2.0 * unit), 2)
        parts, first, one = [high, low, high], 0, 3
    else:
        high, low = pieces(feats, 2)
        parts, first, one = [high, high, low], 3, 0
    spot = lax.broadcasted_iota(jnp.int32, (8, count), 0)
    tail = jnp.where((spot >= one) & (spot < one + 3), 1.0, 0.0)
    for at, part in enumerate(square):
        tail = jnp.where(spot == first + at, part, tail)
    deep = depth_of(width)
    fill = jnp.zeros((deep - 3 * width - 8, count), F32)
    return jnp.concatenate(parts + [tail, fill], axis=0)


def apply(value, eig_ref, how):
    count = value.shape[0]
    both = paired(value)
    wide = lax.dot_general(both, eig_ref[0], how, preferred_element_type=F32)
    slim = lax.dot_general(both[:count], eig_ref[1], how, preferred_element_type=F32)
    return wide[:count] + (wide[count:] + slim)


def depth_of(width):
    return -(-(3 * width + 8) // 128) * 128


def largest(count, limit):
    return max(d for d in range(1, limit + 1) if count % d == 0)


def kmul(a_ref, b_ref, w_ref, o_ref):
    points, outs = a_ref.shape[0], o_ref.shape[0]
    wide = b_ref.shape[1]
    sub = min(512, points)
    parts = largest(points // sub, 3)
    tile = min(512, wide)

    def across(i, unused):
        to = pl.ds(pl.multiple_of(i * tile, tile), tile)
        b = b_ref[:, to]

        def down(j, total):
            for part in range(parts):
                at = pl.ds(pl.multiple_of((j * parts + part) * sub, sub), sub)
                value = jnp.exp2(jnp.dot(a_ref[at, :], b, preferred_element_type=F32))
                high = value.astype(BF16)
                low = (value - high.astype(F32)).astype(BF16)
                w = w_ref[:, at]
                total = total + (
                    jnp.dot(w, high, preferred_element_type=F32)
                    + jnp.dot(w, low, preferred_element_type=F32)
                )
            return total

        total = lax.fori_loop(0, points // (sub * parts), down, jnp.zeros((2 * outs, tile), F32), unroll=True)
        o_ref[:, to] = total[:outs] + total[outs:]
        return unused

    lax.fori_loop(0, wide // tile, across, 0, unroll=True)


def split_of(xs, cs):
    ys = xs if cs % xs == 0 else 1
    return ys, cs // ys


class Place:
    def __init__(self, xs, cs):
        self.xs, self.cs = xs, cs
        self.ys, self.zs = split_of(xs, cs)
        row = lax.axis_index("row")
        self.c = lax.axis_index("col")
        self.k = lax.rem(row, CORES)
        self.x = row // CORES
        self.z, self.y = self.c // self.ys, lax.rem(self.c, self.ys)

    def device(self, k, x, c):
        return (x * CORES + k, c)

    def core(self):
        return [(1 - self.k, self.device(1 - self.k, self.x, self.c))]

    def line(self):
        spots = [lax.rem(self.x + d, self.xs) for d in range(1, self.xs)]
        return [(s, self.device(self.k, s, self.c)) for s in spots]

    def senders(self):
        return [lax.rem(self.x + self.xs - d, self.xs) for d in range(1, self.xs)]

    def cols(self):
        spots = [self.c ^ d for d in range(1, self.cs)]
        return [(s, self.device(self.k, self.x, s)) for s in spots]

    def plane(self):
        found = []
        for d in range(1, self.xs * self.ys):
            x = lax.rem(self.x + d // self.ys, self.xs)
            y = lax.rem(self.y + d % self.ys, self.ys)
            found.append(((x, y), self.device(self.k, x, self.z * self.ys + y)))
        return found

    def across(self):
        spots = [lax.rem(self.y + d, self.ys) for d in range(1, self.ys)]
        return [(s, self.device(self.k, self.x, self.z * self.ys + s)) for s in spots]

    def along(self):
        spots = [lax.rem(self.z + d, self.zs) for d in range(1, self.zs)]
        return [(s, self.device(self.k, self.x, s * self.ys + self.y)) for s in spots]

    def chips(self):
        found = []
        for d in range(1, self.xs * self.cs):
            x, c = lax.rem(self.x + d // self.cs, self.xs), self.c ^ (d % self.cs)
            found.append(((x, c), self.device(self.k, x, c)))
        return found

    def arrive(self):
        sem = pltpu.get_barrier_semaphore()
        everyone = self.core() + self.chips()
        for spot, device in everyone:
            pl.semaphore_signal(sem, inc=1, device_id=device, device_id_type=MESH)
        return lambda: pl.semaphore_wait(sem, len(everyone))


def start(partners, source, target, sems):
    copies = []
    for d, (spot, device) in enumerate(partners):
        copies.append(
            pltpu.make_async_remote_copy(
                src_ref=source(d, spot),
                dst_ref=target(d, spot),
                send_sem=sems[0],
                recv_sem=sems[1],
                device_id=device,
                device_id_type=MESH,
            )
        )
    for copy in copies:
        copy.start()
    return copies


def await_all(whole, sem):
    pltpu.make_async_copy(whole, whole, sem).wait()


def finish(whole, sems):
    for sem in sems:
        await_all(whole, sem)


def summed(first, buffers, count):
    total = first
    for d in range(count):
        total = total + buffers[d]
    return total


def everywhere_steps(place, bufs, sems):
    in_ref, by_core, on_core, by_chip, o_ref = bufs
    k, x, c = place.k, place.x, place.c
    start(place.core(), lambda d, s: in_ref.at[s], lambda d, s: by_core.at[d], sems[0])
    yield
    finish(by_core, sems[0])
    on_core[...] = in_ref[k] + by_core[0]
    start(place.chips(), lambda d, s: on_core.at[s], lambda d, s: by_chip.at[d], sems[1])
    yield
    finish(by_chip, sems[1])
    o_ref[k, x, c] = summed(on_core[x, c], by_chip, by_chip.shape[0])
    start(
        place.chips(), lambda d, s: o_ref.at[k, x, c], lambda d, s: o_ref.at[k, x, c], sems[2]
    )
    yield
    finish(by_chip, sems[2])
    start(place.core(), lambda d, s: o_ref.at[k], lambda d, s: o_ref.at[k], sems[3])
    yield
    finish(by_core, sems[3])


def point_steps(place, bufs, sems):
    in_ref, by_core, on_core, by_plane, on_plane, by_line, o_ref = bufs
    k, x, y, z = place.k, place.x, place.y, place.z
    start(place.core(), lambda d, s: in_ref.at[s], lambda d, s: by_core.at[d], sems[0])
    yield
    finish(by_core, sems[0])
    on_core[...] = in_ref[k] + by_core[0]
    start(place.plane(), lambda d, s: on_core.at[s], lambda d, s: by_plane.at[d], sems[1])
    yield
    finish(by_plane, sems[1])
    on_plane[...] = summed(on_core[x, y], by_plane, by_plane.shape[0])
    start(place.along(), lambda d, s: on_plane.at[s], lambda d, s: by_line.at[d], sems[2])
    yield
    finish(by_line, sems[2])
    o_ref[k, x, y, z] = summed(on_plane[z], by_line, place.zs - 1)
    piece = lambda d, s: o_ref.at[k, x, y, z]
    start(place.along(), piece, piece, sems[3])
    yield
    finish(by_line, sems[3])
    piece = lambda d, s: o_ref.at[k, x, y]
    start(place.across(), piece, piece, sems[4])
    yield
    finish(by_plane.at[pl.ds(0, place.ys - 1)], sems[4])
    piece = lambda d, s: o_ref.at[k, x]
    start(place.line(), piece, piece, sems[5])
    yield
    finish(on_core.at[pl.ds(0, place.xs - 1)], sems[5])
    piece = lambda d, s: o_ref.at[k]
    start(place.core(), piece, piece, sems[6])
    yield
    finish(by_core, sems[6])


def mode_steps(place, bufs, sems, scale_ref, eig_ref):
    part, by_core, on_core, by_line, terms, by_col, o_ref = bufs
    start(place.core(), lambda d, s: part, lambda d, s: by_core.at[d], sems[0])
    yield
    finish(by_core, sems[0])
    on_core[...] = part[...] + by_core[0]
    start(place.line(), lambda d, s: on_core, lambda d, s: by_line.at[d], sems[1])
    yield
    finish(by_line, sems[1])
    coeff = summed(on_core[...], by_line, place.xs - 1) * scale_ref[...]
    correction = apply(coeff, eig_ref, (((1,), (1,)), ((), ())))
    store_tiles(correction, 0, lambda t, tile: place_in(terms, t, tile))
    start(place.cols(), lambda d, s: terms.at[s], lambda d, s: by_col.at[d], sems[2])
    yield
    finish(by_col, sems[2])
    o_ref[place.k, place.x, place.c] = summed(terms[place.c], by_col, place.cs - 1)


def spread(place, o_ref, by_line, by_col, sems, use):
    k, x, c, cs = place.k, place.x, place.c, place.cs
    size = cs // HALVES
    own, own_sent, line, line_sent, near, near_sent, far, far_sent = sems
    halves = [c // size, 1 - c // size]
    part = lambda ref, at: ref.at[pl.ds(at * size, size)]

    def across(d):
        piece = lambda e, s: o_ref.at[k, x, c ^ d]
        start(place.line(), piece, piece, [line_sent.at[0], line.at[d // size]])

    def beside(ref, at, ends):
        piece = lambda d, s: part(ref, at)
        start(place.core(), piece, piece, ends)

    mine = [
        start([partner], lambda d, s: o_ref.at[k, x, c], lambda d, s: o_ref.at[k, x, c], [own_sent.at[0], own.at[d]])
        for d, partner in enumerate(place.cols())
    ]
    across(0)
    for h in range(HALVES):
        for d in range(max(1, h * size), (h + 1) * size):
            await_all(o_ref.at[k, x, c], own.at[d - 1])
            across(d)
        beside(o_ref.at[k, x], halves[h], [near_sent.at[0], near.at[h]])
    for h in range(HALVES):
        use(k, x, halves[h])
    for h in range(HALVES):
        await_all(part(o_ref.at[k, x], 0), near.at[h])
        use(1 - k, x, halves[h])
    for h in range(HALVES):
        await_all(by_line.at[:, pl.ds(0, size)], line.at[h])
        for spot in place.senders():
            beside(o_ref.at[k, spot], halves[h], [far_sent.at[0], far.at[h]])
        for spot in place.senders():
            use(k, spot, halves[h])
    for h in range(HALVES):
        await_all(by_line.at[:, pl.ds(0, size)], far.at[h])
        for spot in place.senders():
            use(1 - k, spot, halves[h])
    await_all(by_col, own_sent.at[0])
    await_all(by_line, line_sent.at[0])
    await_all(o_ref.at[k, x], near_sent.at[0])
    await_all(by_line, far_sent.at[0])


def spot_in(shape, t):
    spots = []
    for count in reversed(shape):
        t, spot = divmod(t, count)
        spots.append(spot)
    return t, tuple(reversed(spots))


def spot_of(shape, t):
    row, spots = spot_in(shape[2:-2], t)
    return (row % CORES, row // CORES) + spots


def place_in(terms, t, tile):
    terms[divmod(t, terms.shape[1])] = tile


def store_tiles(value, block, put):
    high = value.shape[0] // 8
    for j in range(value.shape[1] // 128):
        for g in range(high):
            put((block + j) * high + g, value[8 * g : 8 * g + 8, 128 * j : 128 * j + 128])


def store_all(buf, block, value):
    def put(t, tile):
        buf[spot_of(buf.shape, t)] = tile

    store_tiles(value, block, put)


def load_tiles(get, high, block, blocks):
    columns = []
    for j in range(block, block + blocks):
        columns.append(jnp.concatenate([get(j * high + g) for g in range(high)], axis=0))
    return jnp.concatenate(columns, axis=1) if blocks > 1 else columns[0]


def load_all(buf, high, block, blocks):
    return load_tiles(lambda t: buf[spot_of(buf.shape, t)], high, block, blocks)


def share_of(tiles, xs, cs):
    return -(-tiles // (CORES * xs * cs))


def everywhere_shapes(tiles, xs, cs):
    piece = (share_of(tiles, xs, cs), 8, 128)
    shapes = [
        (CORES, xs, cs) + piece,
        (1, xs, cs) + piece,
        (xs, cs) + piece,
        (xs * cs - 1,) + piece,
        (CORES, xs, cs) + piece,
    ]
    return [pltpu.VMEM(shape, F32) for shape in shapes]


def point_shapes(tiles, xs, cs):
    piece = (share_of(tiles, xs, cs), 8, 128)
    ys, zs = split_of(xs, cs)
    shapes = [
        (CORES, xs, ys, zs) + piece,
        (1, xs, ys, zs) + piece,
        (xs, ys, zs) + piece,
        (xs * ys - 1, zs) + piece,
        (zs,) + piece,
        (zs - 1,) + piece,
        (CORES, xs, ys, zs) + piece,
    ]
    return [pltpu.VMEM(shape, F32) for shape in shapes]


CHUNK = 512


def main_body(
    xs, cs, batch, points, centres_in, weights_in, targets_in, batch_in, points_in, scale_in, eig_in,
    residual, step, *scratch
):
    width, rows = centres_in.shape
    outs = targets_in.shape[0]
    block = eig_in.shape[0]
    some = block // HALVES
    high = width // 8
    scratch = list(scratch)
    take = lambda count: [scratch.pop(0) for i in range(count)]
    pair = lambda count: [[ref.at[0] for ref in take(2)] for i in range(count)]
    b_bufs, p_bufs, m_bufs = take(5), take(5), take(7)
    n_bufs = [take(7) for h in range(HALVES)]
    split, left_rows, batch_right, batch_left, block_high, block_low, pairs, pred = take(8)
    left, kern_high, kern_low = take(3)
    b_sems, p_sems, m_sems = pair(4), pair(4), pair(3)
    n_sems = [pair(7) for h in range(HALVES)]
    spread_sems, input_sems = take(8), take(1)[0]
    by_line = take(1)[0]
    inputs = take(7)
    eig_pair = take(1)[0]
    place = Place(xs, cs)
    k, x, c = place.k, place.x, place.c
    met = place.arrive()
    sources = [centres_in, weights_in, targets_in, batch_in, points_in, scale_in, eig_in]
    loads = [
        pltpu.make_async_copy(source, ref, input_sems.at[i])
        for i, (source, ref) in enumerate(zip(sources, inputs))
    ]
    for i in (0, 3, 4, 1, 2, 5, 6):
        loads[i].start()
    centres, weights, targets, batch_at, points_at, scale, eig = inputs
    offset = lax.axis_index(("row", "col")) * rows

    def pick(index):
        count = index.shape[1]
        spot = lax.broadcasted_iota(jnp.int32, (rows, count), 0)
        hot = jnp.where(spot == index - offset, 1.0, 0.0).astype(BF16)
        got = jnp.dot(split[...], hot, preferred_element_type=F32)
        return (got[:width] + got[width : 2 * width]) + got[2 * width :]

    def pick_points(h, first, last):
        groups = points // block
        for row in range(first * groups // 2, last * groups // 2):
            at = row * block + h * some
            store_all(n_bufs[h][0], row * some // 128, pick(points_at[:, at : at + some]))

    def keep_kernel(first, points_rows):
        count = points_rows.shape[0]
        tile = min(CHUNK, rows)

        def across(i, unused):
            to = pl.ds(pl.multiple_of(i * tile, tile), tile)
            value = jnp.exp2(jnp.dot(points_rows, left[:, to], preferred_element_type=F32))
            near = value.astype(BF16)
            kern_high[pl.ds(first, count), to] = near
            kern_low[pl.ds(first, count), to] = (value - near.astype(F32)).astype(BF16)
            return unused

        lax.fori_loop(0, rows // tile, across, 0, unroll=True)

    def fold(w, first, begin):
        tile = min(CHUNK, rows)
        rest = pl.ds(first, w.shape[1])

        def across(i, unused):
            to = pl.ds(pl.multiple_of(i * tile, tile), tile)
            total = jnp.dot(w, kern_high[rest, to], preferred_element_type=F32)
            total = total + jnp.dot(w, kern_low[rest, to], preferred_element_type=F32)
            total = total[:outs] + total[outs:]
            step[:, to] = total if begin else step[:, to] + total
            return unused

        lax.fori_loop(0, rows // tile, across, 0, unroll=True)

    def row_at(k, x, h):
        return batch + pl.multiple_of((x * CORES + k) * block + h * some, some)

    def feats_of(h, k, x):
        mine = n_bufs[h][6].at[k, x]
        return load_tiles(lambda t: mine[spot_in(mine.shape[:-2], t)[1]], high, 0, some // 128)

    def point_form(h, k, x):
        keep_kernel(row_at(k, x, h), augmented(feats_of(h, k, x), False).T.astype(BF16))

    def own_form(h):
        feats = feats_of(h, k, x)
        form = augmented(feats, False)
        keep_kernel(row_at(k, x, h), form.T.astype(BF16))
        to = slice(h * some, h * some + some)
        value = jnp.exp2(jnp.dot(batch_left[...], form.astype(BF16), preferred_element_type=F32))
        near = value.astype(BF16)
        block_high[:, to] = near
        block_low[:, to] = (value - near.astype(F32)).astype(BF16)

    def use(k, x, h):
        size = cs // HALVES
        mine = m_bufs[6].at[k, x, pl.ds(h * size, size)]
        correction = load_tiles(lambda t: mine[divmod(t, mine.shape[1])], outs // 8, 0, some // 128)
        fold(paired(-learning_rate * correction), row_at(k, x, h), False)

    for bufs in [b_bufs, p_bufs] + n_bufs:
        bufs[0][...] = jnp.zeros_like(bufs[0])
    loads[0].wait()
    loads[3].wait()
    split[...] = jnp.concatenate(pieces(centres[...], 3), axis=0).astype(BF16)
    for at in range(0, batch, CHUNK):
        store_all(b_bufs[0], at // 128, pick(batch_at[:, at : min(at + CHUNK, batch)]))
    loads[4].wait()
    met()
    of_batch = everywhere_steps(place, b_bufs, b_sems)
    of_pred = everywhere_steps(place, p_bufs, p_sems)
    of_points = [point_steps(place, n_bufs[h], n_sems[h]) for h in range(HALVES)]
    next(of_batch)
    pick_points(0, 0, 1)
    next(of_batch)
    pick_points(0, 1, 2)
    next(of_points[0])
    pick_points(1, 0, 2)
    next(of_points[1])
    next(of_points[0])
    next(of_batch)
    next(of_points[1])
    for at in range(0, rows, CHUNK):
        to = slice(at, min(at + CHUNK, rows))
        form = augmented(centres[:, to], True)
        left[:, to] = form.astype(BF16)
        left_rows[to, :] = form.T.astype(BF16)
    for i in (1, 2, 5, 6):
        loads[i].wait()
    pairs[...] = paired(weights[...])
    eig_pair[0], eig_pair[1] = [part.astype(BF16) for part in pieces(eig[...], 2)]
    next(of_points[0])
    next(of_batch)
    next(of_batch, None)

    feats = load_all(b_bufs[4], high, 0, batch // 128)
    form = augmented(feats, False)
    batch_right[...] = form.astype(BF16)
    kmul(left_rows, batch_right, pairs, pred)
    store_all(p_bufs[0], 0, pred[...])
    next(of_pred)
    next(of_points[0])
    next(of_points[1])
    batch_left[...] = augmented(feats, True).T.astype(BF16)
    next(of_pred)
    keep_kernel(0, form.T.astype(BF16))
    next(of_points[0])
    next(of_points[1])
    next(of_pred)
    next(of_points[0])
    own_form(0)
    next(of_points[1])
    next(of_points[1])
    own_form(1)
    next(of_pred)
    next(of_points[0])
    next(of_pred, None)

    rest = load_all(p_bufs[4], outs // 8, 0, batch // 128) - targets[...]
    residual[...] = rest
    pair_rest = paired(rest)
    grad = jnp.dot(pair_rest, block_high[...], preferred_element_type=F32)
    grad = grad + jnp.dot(pair_rest, block_low[...], preferred_element_type=F32)
    m_bufs[0][...] = apply(grad[:outs] + grad[outs:], eig_pair, (((1,), (0,)), ((), ())))
    of_modes = mode_steps(place, m_bufs, m_sems, scale, eig_pair)
    next(of_modes)
    fold(paired(learning_rate * rest), 0, True)
    next(of_modes)
    for spot in place.senders():
        point_form(0, k, spot)
    next(of_points[1])
    next(of_modes)
    for spot in place.senders():
        point_form(1, k, spot)
    next(of_points[0], None)
    for spot in range(xs):
        point_form(0, 1 - k, spot)
    next(of_points[1], None)
    for spot in range(xs):
        point_form(1, 1 - k, spot)
    next(of_modes, None)
    spread(place, m_bufs[6], by_line, m_bufs[5], spread_sems, use)


def local(xs, cs, centres, weights, targets, batch_index, nystrom_index, eigvecs, mode_scale):
    rows, width = centres.shape
    batch, outs = targets.shape
    points = nystrom_index.shape[0]
    block, modes = eigvecs.shape
    deep = depth_of(width)
    total = batch + points
    mode_share = -(-(outs // 8 * block // 128) // cs)
    piece = (mode_share, 8, 128)
    sems = [1] * 2 * (4 + 4 + 3 + 7 * HALVES)
    sems = sems + [cs - 1, 1, HALVES, 1, HALVES, 1, HALVES, 1, 7]
    arrays = [
        centres.T,
        weights.T,
        targets.T,
        batch_index[None, :],
        nystrom_index[None, :],
        mode_scale[None, :],
        eigvecs,
    ]
    residual, step = pl.pallas_call(
        functools.partial(main_body, xs, cs, batch, points),
        out_shape=[pltpu.VMEM((outs, batch), F32), pltpu.VMEM((outs, rows), F32)],
        in_specs=[pl.BlockSpec(memory_space=pl.ANY)] * 7,
        out_specs=[VMEM] * 2,
        scratch_shapes=everywhere_shapes(width // 8 * batch // 128, xs, cs)
        + everywhere_shapes(outs // 8 * batch // 128, xs, cs)
        + [
            pltpu.VMEM((outs, modes), F32),
            pltpu.VMEM((1, outs, modes), F32),
            pltpu.VMEM((outs, modes), F32),
            pltpu.VMEM((xs - 1, outs, modes), F32),
            pltpu.VMEM((cs,) + piece, F32),
            pltpu.VMEM((cs - 1,) + piece, F32),
            pltpu.VMEM((CORES, xs, cs) + piece, F32),
        ]
        + point_shapes(width // 8 * points // HALVES // 128, xs, cs) * HALVES
        + [
            pltpu.VMEM((3 * width, rows), BF16),
            pltpu.VMEM((rows, deep), BF16),
            pltpu.VMEM((deep, batch), BF16),
            pltpu.VMEM((batch, deep), BF16),
            pltpu.VMEM((batch, block), BF16),
            pltpu.VMEM((batch, block), BF16),
            pltpu.VMEM((2 * outs, rows), BF16),
            pltpu.VMEM((outs, batch), F32),
            pltpu.VMEM((deep, rows), BF16),
            pltpu.VMEM((total, rows), BF16),
            pltpu.VMEM((total, rows), BF16),
        ]
        + [pltpu.SemaphoreType.DMA((n,)) for n in sems]
        + [pltpu.VMEM((xs - 1, cs) + piece, F32)]
        + [pltpu.VMEM(array.shape, array.dtype) for array in arrays]
        + [pltpu.VMEM((2, block, modes), BF16)],
        compiler_params=pltpu.CompilerParams(
            collective_id=0, has_side_effects=True, vmem_limit_bytes=65_500_000
        ),
    )(*arrays)
    return (residual.T, step.T)


def solution(mesh):
    in_specs = (
        P(("row", "col"), None),
        P(("row", "col"), None),
        P(),
        P(),
        P(),
        P("row", "col"),
        P("col"),
    )
    out_specs = (P(), P(("row", "col"), None))
    body = functools.partial(local, mesh.shape["row"] // CORES, mesh.shape["col"])
    return jax.shard_map(body, mesh=mesh, in_specs=in_specs, out_specs=out_specs, check_vma=False)
```

profile of v0, /device:TPU:0, one launch (start us, length us, event | category | flops | bytes accessed | tf_op | source)
XLA Modules:
  0.0 61.7 jit_solution(14042205818057688062)
XLA Ops:
  0.6 59.6 %shard_map.86 = (f32[64,512]{1,0:T(8,128)S(1)}, f32[64,2048]{1,0:T(8,128)S(1)}) custom-call(f32[64,2048]{1,0:T(8,128)} %bitcast.10, f32[64,2048]{1,0:T(8,128)} %bitcast.11, f32[64,512]{1,0:T(8,128)} %bitcast.12, s32[1,512]{1,0:T(1,128)} %bitcast.14, s32[1,4096]{1,0:T(1,128)} %bitcast.13, f32[1,128]{1,0:T(1,128)} %bitcast.15, f32[1024,128]{1,0:T(8,128)} %eig_in.1), custom_call_target="tpu_custom_call" | custom-call | tf_op jit(solution)/shard_map/pallas_call | solution.py:596
  60.3 0.7 %copy.11 = f32[512,64]{0,1:T(8,128)} copy(f32[512,64]{0,1:T(8,128)S(1)} %bitcast.9) | data formatting | bytes 262144
  60.9 0.8 %copy.12 = f32[2048,64]{0,1:T(8,128)} copy(f32[2048,64]{0,1:T(8,128)S(1)} %bitcast.8) | data formatting | bytes 1048576
where the time goes:
time: 61.9 us; the launch traced here: 61.7 us
  Pallas kernels  59.6 us (96%)
  local copies, waits for them, and re-layouts  1.45 us (2%)
  between operations  0.64 us (1%)
    pallas_call x1, Pallas kernels, local(): pl.pallas_call(functools.partial(main_body, xs, cs, batch, points), out_s...  59.6 us
    unnamed x2, local copies, waits for them, and re-layouts  1.45 us

commit v1 on v0

--- a/solution.py
+++ b/solution.py
@@ -121,6 +121,13 @@
         spots = [lax.rem(self.x + d, self.xs) for d in range(1, self.xs)]
         return [(s, self.device(self.k, s, self.c)) for s in spots]
 
+    def row(self):
+        found = []
+        for d in range(1, self.xs * CORES):
+            x, k = lax.rem(self.x + d // CORES, self.xs), lax.rem(self.k + d % CORES, CORES)
+            found.append(((k, x), self.device(k, x, self.c)))
+        return found[::-1]
+
     def senders(self):
         return [lax.rem(self.x + self.xs - d, self.xs) for d in range(1, self.xs)]
 
@@ -134,7 +141,7 @@
             x = lax.rem(self.x + d // self.ys, self.xs)
             y = lax.rem(self.y + d % self.ys, self.ys)
             found.append(((x, y), self.device(self.k, x, self.z * self.ys + y)))
-        return found
+        return found[::-1]
 
     def across(self):
         spots = [lax.rem(self.y + d, self.ys) for d in range(1, self.ys)]
@@ -149,7 +156,7 @@
         for d in range(1, self.xs * self.cs):
             x, c = lax.rem(self.x + d // self.cs, self.xs), self.c ^ (d % self.cs)
             found.append(((x, c), self.device(self.k, x, c)))
-        return found
+        return found[::-1]
 
     def arrive(self):
         sem = pltpu.get_barrier_semaphore()
@@ -248,20 +255,16 @@
 
 
 def mode_steps(place, bufs, sems, scale_ref, eig_ref):
-    part, by_core, on_core, by_line, terms, by_col, o_ref = bufs
-    start(place.core(), lambda d, s: part, lambda d, s: by_core.at[d], sems[0])
-    yield
-    finish(by_core, sems[0])
-    on_core[...] = part[...] + by_core[0]
-    start(place.line(), lambda d, s: on_core, lambda d, s: by_line.at[d], sems[1])
-    yield
-    finish(by_line, sems[1])
-    coeff = summed(on_core[...], by_line, place.xs - 1) * scale_ref[...]
+    part, by_row, terms, by_col, o_ref = bufs
+    start(place.row(), lambda d, s: part, lambda d, s: by_row.at[d], sems[0])
+    yield
+    finish(by_row, sems[0])
+    coeff = summed(part[...], by_row, by_row.shape[0]) * scale_ref[...]
     correction = apply(coeff, eig_ref, (((1,), (1,)), ((), ())))
     store_tiles(correction, 0, lambda t, tile: place_in(terms, t, tile))
-    start(place.cols(), lambda d, s: terms.at[s], lambda d, s: by_col.at[d], sems[2])
-    yield
-    finish(by_col, sems[2])
+    start(place.cols(), lambda d, s: terms.at[s], lambda d, s: by_col.at[d], sems[1])
+    yield
+    finish(by_col, sems[1])
     o_ref[place.k, place.x, place.c] = summed(terms[place.c], by_col, place.cs - 1)
 
 
@@ -290,7 +293,6 @@
             await_all(o_ref.at[k, x, c], own.at[d - 1])
             across(d)
         beside(o_ref.at[k, x], halves[h], [near_sent.at[0], near.at[h]])
-    for h in range(HALVES):
         use(k, x, halves[h])
     for h in range(HALVES):
         await_all(part(o_ref.at[k, x], 0), near.at[h])
@@ -301,7 +303,6 @@
             beside(o_ref.at[k, spot], halves[h], [far_sent.at[0], far.at[h]])
         for spot in place.senders():
             use(k, spot, halves[h])
-    for h in range(HALVES):
         await_all(by_line.at[:, pl.ds(0, size)], far.at[h])
         for spot in place.senders():
             use(1 - k, spot, halves[h])
@@ -399,11 +400,11 @@
     scratch = list(scratch)
     take = lambda count: [scratch.pop(0) for i in range(count)]
     pair = lambda count: [[ref.at[0] for ref in take(2)] for i in range(count)]
-    b_bufs, p_bufs, m_bufs = take(5), take(5), take(7)
+    b_bufs, p_bufs, m_bufs = take(5), take(5), take(5)
     n_bufs = [take(7) for h in range(HALVES)]
     split, left_rows, batch_right, batch_left, block_high, block_low, pairs, pred = take(8)
     left, kern_high, kern_low = take(3)
-    b_sems, p_sems, m_sems = pair(4), pair(4), pair(3)
+    b_sems, p_sems, m_sems = pair(4), pair(4), pair(2)
     n_sems = [pair(7) for h in range(HALVES)]
     spread_sems, input_sems = take(8), take(1)[0]
     by_line = take(1)[0]
@@ -474,9 +475,7 @@
         keep_kernel(row_at(k, x, h), augmented(feats_of(h, k, x), False).T.astype(BF16))
 
     def own_form(h):
-        feats = feats_of(h, k, x)
-        form = augmented(feats, False)
-        keep_kernel(row_at(k, x, h), form.T.astype(BF16))
+        form = augmented(feats_of(h, k, x), False)
         to = slice(h * some, h * some + some)
         value = jnp.exp2(jnp.dot(batch_left[...], form.astype(BF16), preferred_element_type=F32))
         near = value.astype(BF16)
@@ -485,7 +484,7 @@
 
     def use(k, x, h):
         size = cs // HALVES
-        mine = m_bufs[6].at[k, x, pl.ds(h * size, size)]
+        mine = m_bufs[4].at[k, x, pl.ds(h * size, size)]
         correction = load_tiles(lambda t: mine[divmod(t, mine.shape[1])], outs // 8, 0, some // 128)
         fold(paired(-learning_rate * correction), row_at(k, x, h), False)
 
@@ -522,6 +521,7 @@
     eig_pair[0], eig_pair[1] = [part.astype(BF16) for part in pieces(eig[...], 2)]
     next(of_points[0])
     next(of_batch)
+    next(of_points[1])
     next(of_batch, None)
 
     feats = load_all(b_bufs[4], high, 0, batch // 128)
@@ -531,20 +531,20 @@
     store_all(p_bufs[0], 0, pred[...])
     next(of_pred)
     next(of_points[0])
-    next(of_points[1])
     batch_left[...] = augmented(feats, True).T.astype(BF16)
     next(of_pred)
+    next(of_points[1])
     keep_kernel(0, form.T.astype(BF16))
     next(of_points[0])
+    next(of_pred)
     next(of_points[1])
-    next(of_pred)
     next(of_points[0])
     own_form(0)
-    next(of_points[1])
+    point_form(0, k, x)
     next(of_points[1])
     own_form(1)
     next(of_pred)
-    next(of_points[0])
+    point_form(1, k, x)
     next(of_pred, None)
 
     rest = load_all(p_bufs[4], outs // 8, 0, batch // 128) - targets[...]
@@ -555,8 +555,8 @@
     m_bufs[0][...] = apply(grad[:outs] + grad[outs:], eig_pair, (((1,), (0,)), ((), ())))
     of_modes = mode_steps(place, m_bufs, m_sems, scale, eig_pair)
     next(of_modes)
+    next(of_points[0])
     fold(paired(learning_rate * rest), 0, True)
-    next(of_modes)
     for spot in place.senders():
         point_form(0, k, spot)
     next(of_points[1])
@@ -570,7 +570,7 @@
     for spot in range(xs):
         point_form(1, 1 - k, spot)
     next(of_modes, None)
-    spread(place, m_bufs[6], by_line, m_bufs[5], spread_sems, use)
+    spread(place, m_bufs[4], by_line, m_bufs[3], spread_sems, use)
 
 
 def local(xs, cs, centres, weights, targets, batch_index, nystrom_index, eigvecs, mode_scale):
@@ -582,7 +582,7 @@
     total = batch + points
     mode_share = -(-(outs // 8 * block // 128) // cs)
     piece = (mode_share, 8, 128)
-    sems = [1] * 2 * (4 + 4 + 3 + 7 * HALVES)
+    sems = [1] * 2 * (4 + 4 + 2 + 7 * HALVES)
     sems = sems + [cs - 1, 1, HALVES, 1, HALVES, 1, HALVES, 1, 7]
     arrays = [
         centres.T,
@@ -602,9 +602,7 @@
         + everywhere_shapes(outs // 8 * batch // 128, xs, cs)
         + [
             pltpu.VMEM((outs, modes), F32),
-            pltpu.VMEM((1, outs, modes), F32),
-            pltpu.VMEM((outs, modes), F32),
-            pltpu.VMEM((xs - 1, outs, modes), F32),
+            pltpu.VMEM((CORES * xs - 1, outs, modes), F32),
             pltpu.VMEM((cs,) + piece, F32),
             pltpu.VMEM((cs - 1,) + piece, F32),
             pltpu.VMEM((CORES, xs, cs) + piece, F32),

time: 61.9 us -> 58.8 us (0.950)
  Pallas kernels: 59.6 us -> 56.5 us
    pallas_call x1, Pallas kernels: 59.6 us -> 56.5 us  [local(): pl.pallas_call(functools.partial(main_body, xs, cs, batch, points), out_s...]
where the time goes in v1:
time: 58.8 us; the launch traced here: 58.6 us
  Pallas kernels  56.5 us (96%)
  local copies, waits for them, and re-layouts  1.45 us (2%)
  between operations  0.64 us (1%)
    pallas_call x1, Pallas kernels, local(): pl.pallas_call(functools.partial(main_body, xs, cs, batch, points), out_s...  56.5 us
    unnamed x2, local copies, waits for them, and re-layouts  1.45 us

profile of v1, /device:TPU:0, one launch (start us, length us, event | category | flops | bytes accessed | tf_op | source)
XLA Modules:
  0.0 58.6 jit_solution(3610047947474252569)
XLA Ops:
  0.6 56.5 %shard_map.86 = (f32[64,512]{1,0:T(8,128)S(1)}, f32[64,2048]{1,0:T(8,128)S(1)}) custom-call(f32[64,2048]{1,0:T(8,128)} %bitcast.10, f32[64,2048]{1,0:T(8,128)} %bitcast.11, f32[64,512]{1,0:T(8,128)} %bitcast.12, s32[1,512]{1,0:T(1,128)} %bitcast.14, s32[1,4096]{1,0:T(1,128)} %bitcast.13, f32[1,128]{1,0:T(1,128)} %bitcast.15, f32[1024,128]{1,0:T(8,128)} %eig_in.1), custom_call_target="tpu_custom_call" | custom-call | tf_op jit(solution)/shard_map/pallas_call | solution.py:596
  57.2 0.7 %copy.11 = f32[512,64]{0,1:T(8,128)} copy(f32[512,64]{0,1:T(8,128)S(1)} %bitcast.9) | data formatting | bytes 262144
  57.8 0.8 %copy.12 = f32[2048,64]{0,1:T(8,128)} copy(f32[2048,64]{0,1:T(8,128)S(1)} %bitcast.8) | data formatting | bytes 1048576

commit v2 on v1

--- a/solution.py
+++ b/solution.py
@@ -65,35 +65,21 @@
     return max(d for d in range(1, limit + 1) if count % d == 0)
 
 
-def kmul(a_ref, b_ref, w_ref, o_ref):
-    points, outs = a_ref.shape[0], o_ref.shape[0]
-    wide = b_ref.shape[1]
+def kmul(a_ref, b, w_ref):
+    points, outs = a_ref.shape[0], w_ref.shape[0] // 2
     sub = min(512, points)
-    parts = largest(points // sub, 3)
-    tile = min(512, wide)
-
-    def across(i, unused):
-        to = pl.ds(pl.multiple_of(i * tile, tile), tile)
-        b = b_ref[:, to]
-
-        def down(j, total):
-            for part in range(parts):
-                at = pl.ds(pl.multiple_of((j * parts + part) * sub, sub), sub)
-                value = jnp.exp2(jnp.dot(a_ref[at, :], b, preferred_element_type=F32))
-                high = value.astype(BF16)
-                low = (value - high.astype(F32)).astype(BF16)
-                w = w_ref[:, at]
-                total = total + (
-                    jnp.dot(w, high, preferred_element_type=F32)
-                    + jnp.dot(w, low, preferred_element_type=F32)
-                )
-            return total
-
-        total = lax.fori_loop(0, points // (sub * parts), down, jnp.zeros((2 * outs, tile), F32), unroll=True)
-        o_ref[:, to] = total[:outs] + total[outs:]
-        return unused
-
-    lax.fori_loop(0, wide // tile, across, 0, unroll=True)
+    total = jnp.zeros((2 * outs, b.shape[1]), F32)
+    for part in range(points // sub):
+        at = slice(part * sub, part * sub + sub)
+        value = jnp.exp2(jnp.dot(a_ref[at, :], b, preferred_element_type=F32))
+        high = value.astype(BF16)
+        low = (value - high.astype(F32)).astype(BF16)
+        w = w_ref[:, at]
+        total = total + (
+            jnp.dot(w, high, preferred_element_type=F32)
+            + jnp.dot(w, low, preferred_element_type=F32)
+        )
+    return total[:outs] + total[outs:]
 
 
 def split_of(xs, cs):
@@ -260,7 +246,7 @@
     yield
     finish(by_row, sems[0])
     coeff = summed(part[...], by_row, by_row.shape[0]) * scale_ref[...]
-    correction = apply(coeff, eig_ref, (((1,), (1,)), ((), ())))
+    correction = apply(coeff, eig_ref, (((1,), (0,)), ((), ())))
     store_tiles(correction, 0, lambda t, tile: place_in(terms, t, tile))
     start(place.cols(), lambda d, s: terms.at[s], lambda d, s: by_col.at[d], sems[1])
     yield
@@ -320,9 +306,10 @@
     return t, tuple(reversed(spots))
 
 
-def spot_of(shape, t):
+def spot_of(shape, t, other=False):
     row, spots = spot_in(shape[2:-2], t)
-    return (row % CORES, row // CORES) + spots
+    core = row % CORES
+    return (1 - core if other else core, row // CORES) + spots
 
 
 def place_in(terms, t, tile):
@@ -336,9 +323,9 @@
             put((block + j) * high + g, value[8 * g : 8 * g + 8, 128 * j : 128 * j + 128])
 
 
-def store_all(buf, block, value):
+def store_all(buf, block, value, other=False):
     def put(t, tile):
-        buf[spot_of(buf.shape, t)] = tile
+        buf[spot_of(buf.shape, t, other)] = tile
 
     store_tiles(value, block, put)
 
@@ -350,8 +337,8 @@
     return jnp.concatenate(columns, axis=1) if blocks > 1 else columns[0]
 
 
-def load_all(buf, high, block, blocks):
-    return load_tiles(lambda t: buf[spot_of(buf.shape, t)], high, block, blocks)
+def load_all(buf, high, block, blocks, other=False):
+    return load_tiles(lambda t: buf[spot_of(buf.shape, t, other)], high, block, blocks)
 
 
 def share_of(tiles, xs, cs):
@@ -397,19 +384,21 @@
     block = eig_in.shape[0]
     some = block // HALVES
     high = width // 8
+    tiles_of = lambda rows: cs * share_of(rows // 8 * batch // 128, xs, cs)
+    by_block = batch // 128 == CORES * xs and tiles_of(width) == high and tiles_of(outs) == outs // 8
     scratch = list(scratch)
     take = lambda count: [scratch.pop(0) for i in range(count)]
     pair = lambda count: [[ref.at[0] for ref in take(2)] for i in range(count)]
     b_bufs, p_bufs, m_bufs = take(5), take(5), take(5)
     n_bufs = [take(7) for h in range(HALVES)]
-    split, left_rows, batch_right, batch_left, block_high, block_low, pairs, pred = take(8)
+    split, left_rows, batch_left, block_high, block_low, pairs = take(6)
     left, kern_high, kern_low = take(3)
     b_sems, p_sems, m_sems = pair(4), pair(4), pair(2)
     n_sems = [pair(7) for h in range(HALVES)]
     spread_sems, input_sems = take(8), take(1)[0]
     by_line = take(1)[0]
     inputs = take(7)
-    eig_pair = take(1)[0]
+    eig_pair, eig_turned = take(2)
     place = Place(xs, cs)
     k, x, c = place.k, place.x, place.c
     met = place.arrive()
@@ -505,9 +494,10 @@
     next(of_batch)
     pick_points(0, 1, 2)
     next(of_points[0])
-    pick_points(1, 0, 2)
+    pick_points(1, 0, 1)
+    next(of_points[0])
+    pick_points(1, 1, 2)
     next(of_points[1])
-    next(of_points[0])
     next(of_batch)
     next(of_points[1])
     for at in range(0, rows, CHUNK):
@@ -519,44 +509,61 @@
         loads[i].wait()
     pairs[...] = paired(weights[...])
     eig_pair[0], eig_pair[1] = [part.astype(BF16) for part in pieces(eig[...], 2)]
+    eig_turned[0], eig_turned[1] = [part.astype(BF16) for part in pieces(eig[...].T, 2)]
     next(of_points[0])
     next(of_batch)
-    next(of_points[1])
-    next(of_batch, None)
-
-    feats = load_all(b_bufs[4], high, 0, batch // 128)
-    form = augmented(feats, False)
-    batch_right[...] = form.astype(BF16)
-    kmul(left_rows, batch_right, pairs, pred)
-    store_all(p_bufs[0], 0, pred[...])
-    next(of_pred)
-    next(of_points[0])
-    batch_left[...] = augmented(feats, True).T.astype(BF16)
-    next(of_pred)
-    next(of_points[1])
-    keep_kernel(0, form.T.astype(BF16))
-    next(of_points[0])
+    if by_block:
+        for first, half in ((True, k), (False, 1 - k)):
+            if not first:
+                next(of_batch, None)
+            blocks = [b_bufs[4].at[half, spot] for spot in range(xs)]
+            get = [lambda t, ref=ref: ref[spot_in(ref.shape[:-2], t)[1]] for ref in blocks]
+            feats = jnp.concatenate([load_tiles(one, high, 0, 1) for one in get], axis=1)
+            part = kmul(left_rows, augmented(feats, False).astype(BF16), pairs)
+            for spot in range(xs):
+                into = p_bufs[0].at[1 - half, spot]
+
+                def put(t, tile):
+                    into[spot_in(into.shape[:-2], t)[1]] = tile
+
+                store_tiles(part[:, spot * 128 : spot * 128 + 128], 0, put)
+            if first:
+                next(of_pred)
+    else:
+        next(of_batch, None)
+        feats = load_all(b_bufs[4], high, 0, batch // 128)
+        store_all(p_bufs[0], 0, kmul(left_rows, augmented(feats, False).astype(BF16), pairs), by_block)
+        next(of_pred)
     next(of_pred)
     next(of_points[1])
     next(of_points[0])
+    feats = load_all(b_bufs[4], high, 0, batch // 128)
+    form = augmented(feats, False)
+    batch_left[...] = augmented(feats, True).T.astype(BF16)
+    keep_kernel(0, form.T.astype(BF16))
+    next(of_pred)
+    next(of_points[1])
+    next(of_points[0])
+    next(of_points[1])
+    next(of_points[0])
     own_form(0)
+    next(of_pred)
     point_form(0, k, x)
     next(of_points[1])
     own_form(1)
-    next(of_pred)
-    point_form(1, k, x)
     next(of_pred, None)
 
-    rest = load_all(p_bufs[4], outs // 8, 0, batch // 128) - targets[...]
+    rest = load_all(p_bufs[4], outs // 8, 0, batch // 128, by_block) - targets[...]
     residual[...] = rest
     pair_rest = paired(rest)
     grad = jnp.dot(pair_rest, block_high[...], preferred_element_type=F32)
     grad = grad + jnp.dot(pair_rest, block_low[...], preferred_element_type=F32)
     m_bufs[0][...] = apply(grad[:outs] + grad[outs:], eig_pair, (((1,), (0,)), ((), ())))
-    of_modes = mode_steps(place, m_bufs, m_sems, scale, eig_pair)
+    of_modes = mode_steps(place, m_bufs, m_sems, scale, eig_turned)
     next(of_modes)
     next(of_points[0])
     fold(paired(learning_rate * rest), 0, True)
+    point_form(1, k, x)
     for spot in place.senders():
         point_form(0, k, spot)
     next(of_points[1])
@@ -611,12 +618,10 @@
         + [
             pltpu.VMEM((3 * width, rows), BF16),
             pltpu.VMEM((rows, deep), BF16),
-            pltpu.VMEM((deep, batch), BF16),
             pltpu.VMEM((batch, deep), BF16),
             pltpu.VMEM((batch, block), BF16),
             pltpu.VMEM((batch, block), BF16),
             pltpu.VMEM((2 * outs, rows), BF16),
-            pltpu.VMEM((outs, batch), F32),
             pltpu.VMEM((deep, rows), BF16),
             pltpu.VMEM((total, rows), BF16),
             pltpu.VMEM((total, rows), BF16),
@@ -624,7 +629,7 @@
         + [pltpu.SemaphoreType.DMA((n,)) for n in sems]
         + [pltpu.VMEM((xs - 1, cs) + piece, F32)]
         + [pltpu.VMEM(array.shape, array.dtype) for array in arrays]
-        + [pltpu.VMEM((2, block, modes), BF16)],
+        + [pltpu.VMEM((2, block, modes), BF16), pltpu.VMEM((2, modes, block), BF16)],
         compiler_params=pltpu.CompilerParams(
             collective_id=0, has_side_effects=True, vmem_limit_bytes=65_500_000
         ),

time: 58.8 us -> 58.4 us (level)
  no operation moved by 1% of the time
where the time goes in v2:
time: 58.4 us; the launch traced here: 58.3 us
  Pallas kernels  56.2 us (96%)
  local copies, waits for them, and re-layouts  1.45 us (2%)
  between operations  0.64 us (1%)
    pallas_call x1, Pallas kernels, local(): pl.pallas_call(functools.partial(main_body, xs, cs, batch, points), out_s...  56.2 us
    unnamed x2, local copies, waits for them, and re-layouts  1.45 us

profile of v2, /device:TPU:0, one launch (start us, length us, event | category | flops | bytes accessed | tf_op | source)
XLA Modules:
  0.0 58.3 jit_solution(12869240906983366777)
XLA Ops:
  0.6 56.2 %shard_map.86 = (f32[64,512]{1,0:T(8,128)S(1)}, f32[64,2048]{1,0:T(8,128)S(1)}) custom-call(f32[64,2048]{1,0:T(8,128)} %bitcast.10, f32[64,2048]{1,0:T(8,128)} %bitcast.11, f32[64,512]{1,0:T(8,128)} %bitcast.12, s32[1,512]{1,0:T(1,128)} %bitcast.14, s32[1,4096]{1,0:T(1,128)} %bitcast.13, f32[1,128]{1,0:T(1,128)} %bitcast.15, f32[1024,128]{1,0:T(8,128)} %eig_in.1), custom_call_target="tpu_custom_call" | custom-call | tf_op jit(solution)/shard_map/pallas_call | solution.py:603
  56.8 0.7 %copy.11 = f32[512,64]{0,1:T(8,128)} copy(f32[512,64]{0,1:T(8,128)S(1)} %bitcast.9) | data formatting | bytes 262144
  57.5 0.8 %copy.12 = f32[2048,64]{0,1:T(8,128)} copy(f32[2048,64]{0,1:T(8,128)S(1)} %bitcast.8) | data formatting | bytes 1048576
